TPU v7x, 128 devices: a whole 4x4x4 slice. The times are simulated.
128 devices in a mesh: ax: 16 (over x, z), rad: 8 (over y, core).
Axes of the slice: x: 4, y: 4, z: 4, core: 2. Of those that a mesh axis runs over, the one named last changes fastest.
Arguments:
- forcing: float32 [32, 5, 256, 1024], P(None, None, 'ax', 'rad'), may hold values from -300 to 300, as said below
- vel_axial: float32 [256, 1024], P('ax', 'rad'), may hold values from 0.2 to 1
- vel_radial: float32 [256, 1024], P('ax', 'rad'), may hold values from -0.4 to 0.4
- coupling: float32 [5, 5, 256, 1024], P(None, None, 'ax', 'rad'), may hold values from -1.5 to 1.5
- viscosity: float32 [5], replicated, may hold values from 0.03 to 0.18
Outputs:
- basis: float32 [32, 5, 256, 1024], P(None, None, 'ax', 'rad')
- r_factor: float32 [32, 32], replicated
Inputs may be any that keep to these rules, and one draw needn't show every extreme that they name: `forcing`: forcing of the linearized equations.
All inputs are finite; a program needn't handle non-finite values.
Results may differ from a plain program's by a relative error of at most 0.00024.
Values sent between devices are 32-bit elements; how exact they have to be, the bound alone decides.
No kernel may reach another device: no remote copies, remote signals or barrier semaphores. Data moves between devices by JAX's collectives and lax.ppermute only.
A program may use at most 64 MiB of HBM per device.

v0:
```python
import jax
import jax.numpy as jnp
from jax import lax
from jax.sharding import PartitionSpec as P

STEPS = 3
time_step = 0.8


def padded_2(shard, sides, width):
    for axis, dim in sides:
        size, length = (lax.axis_size(axis), shard.shape[dim])
        up = [(i, (i + 1) % size) for i in range(size - 1)]
        down = [(j, i) for i, j in up]
        last = lax.slice_in_dim(shard, length - width, length, axis=dim)
        initial = lax.slice_in_dim(shard, 0, width, axis=dim)
        before = lax.ppermute(last, axis, up)
        after = lax.ppermute(initial, axis, down)
        shard = jnp.concatenate([before, shard, after], axis=dim)
    return shard


def combined_all(shard, axis, combine):
    everything = lax.all_gather(shard, axis)
    initial = everything[0]

    def turn(k, so_far):
        return combine(so_far, everything[k])

    return lax.fori_loop(1, lax.axis_size(axis), turn, initial)


def operate(padded, vel_axial, vel_radial, coupling, viscosity):
    center = padded[..., 2:-2, 2:-2]
    axial_up = padded[..., 3:-1, 2:-2]
    axial_down = padded[..., 1:-3, 2:-2]
    axial_far_up = padded[..., 4:, 2:-2]
    axial_far_down = padded[..., :-4, 2:-2]
    radial_up = padded[..., 2:-2, 3:-1]
    radial_down = padded[..., 2:-2, 1:-3]
    radial_far_up = padded[..., 2:-2, 4:]
    radial_far_down = padded[..., 2:-2, :-4]
    first_axial = (8.0 * (axial_up - axial_down) - (axial_far_up - axial_far_down)) / 12.0
    first_radial = (8.0 * (radial_up - radial_down) - (radial_far_up - radial_far_down)) / 12.0
    second = (
        16.0 * (axial_up + axial_down + radial_up + radial_down)
        - (axial_far_up + axial_far_down + radial_far_up + radial_far_down)
        - 60.0 * center
    ) / 12.0
    result = (
        -vel_axial * first_axial - vel_radial * first_radial + viscosity[:, None, None] * second
    )
    for source in range(coupling.shape[1]):
        result = result + coupling[:, source] * center[..., source : source + 1, :, :]
    return result


def upper_inverse(upper_factor):
    order = upper_factor.shape[0]
    identity = jnp.eye(order, dtype=jnp.float32)

    def one_row(count, inverse):
        row_index = order - 1 - count
        factor_row = lax.dynamic_slice_in_dim(upper_factor, row_index, 1, 0)
        unit_row = lax.dynamic_slice_in_dim(identity, row_index, 1, 0)
        pivot = jnp.sum(factor_row * unit_row)
        new_row = (unit_row - jnp.dot(factor_row, inverse, precision=lax.Precision.HIGHEST)) / pivot
        return lax.dynamic_update_slice_in_dim(inverse, new_row, row_index, 0)

    return lax.fori_loop(0, order, one_row, jnp.zeros((order, order), jnp.float32))


def rim_operator(field_now, vel_axial, vel_radial, coupling, viscosity):
    padded = padded_2(field_now, (("ax", 2), ("rad", 3)), 2)
    return operate(padded, vel_axial, vel_radial, coupling, viscosity)


def join_factors(first_factor, other_factor):
    summed = jnp.dot(first_factor.T, first_factor, precision=lax.Precision.HIGHEST)
    summed = summed + jnp.dot(other_factor.T, other_factor, precision=lax.Precision.HIGHEST)
    return jnp.linalg.cholesky(summed).T


def per_device(forcing, vel_axial, vel_radial, coupling, viscosity):
    vectors, variables, axial_cells, radial_cells = forcing.shape
    field_now = forcing
    for step_index in range(STEPS):
        slope_one = rim_operator(field_now, vel_axial, vel_radial, coupling, viscosity)
        middle = field_now + time_step * slope_one
        slope_two = rim_operator(middle, vel_axial, vel_radial, coupling, viscosity)
        field_now = field_now + 0.5 * time_step * (slope_one + slope_two)
    flattened = field_now.reshape(vectors, variables * axial_cells * radial_cells)
    rows_all = variables * axial_cells * radial_cells * lax.axis_size("ax") * lax.axis_size("rad")
    local_gram = jnp.dot(flattened, flattened.T, precision=lax.Precision.HIGHEST) / rows_all
    radial_gram = lax.psum(local_gram, "rad")
    start_factor = jnp.linalg.cholesky(radial_gram).T
    upper_factor = combined_all(start_factor, "ax", join_factors)
    inverse = upper_inverse(upper_factor)
    basis = jnp.dot(inverse.T, flattened, precision=lax.Precision.HIGHEST).reshape(field_now.shape)
    return (basis, upper_factor)


def solution(mesh):
    return jax.shard_map(
        per_device,
        mesh=mesh,
        in_specs=(
            P(None, None, "ax", "rad"),
            P("ax", "rad"),
            P("ax", "rad"),
            P(None, None, "ax", "rad"),
            P(),
        ),
        out_specs=(P(None, None, "ax", "rad"), P()),
        check_vma=False,
    )
```

profile of v0, /device:TPU:0, one launch (start us, length us, event | category | flops | bytes accessed | tf_op | source)
XLA Modules:
  0.0 470.0 jit_solution(13325855620133303022)
XLA Ops:
  2.8 4.6 collective-permute-start.1
  9.4 4.3 copy.227
  19.7 3.5 pad_maximum_fusion
  23.2 3.1 copy-done.1
  35.9 6.5 %copy.229 = f32[32,5,20,128]{3,0,2,1:T(8,128)} copy(f32[32,5,20,128]{0,2,3,1:T(8,128)} %copy-done.1) | data formatting | bytes 3276800 | tf_op jit(solution)/shard_map/concatenate | solution.py:19
  46.1 8.8 %multiply_add_fusion.7 = (f32[32,5,16,128]{3,0,2,1:T(8,128)S(1)}, f32[32,5,16,128]{3,0,2,1:T(8,128)}) fusion(f32[32,5,16,128]{3,2,1,0:T(8,128)S(1)} %copy-done, f32[32,16,128]{2,0,1:T(8,128)} %copy.238, f32[5,16,128]{2,1,0:T(8,128)S(1)} %get-tuple-element.336, f32[32,16,128]{2,0,1:T(8,128)} %copy.237, f32[5,16,128]{2,1,0:T(8,128)S(1)} %get-tuple-element.337, ...), kind=kLoop, calls=%fused_computation.117 | loop fusion | flops 12779520 | bytes 12396564 | tf_op jit(solution)/shard_map/add | solution.py:89
  56.3 5.2 %collective-permute-start.5 = (f32[32,5,2,128]{3,0,2,1:T(8,128)S(1)}, f32[32,5,2,128]{3,0,2,1:T(8,128)S(1)}, u32[]{:S(2)}, u32[]{:S(2)}) collective-permute-start(f32[32,5,2,128]{3,0,2,1:T(8,128)S(1)} %get-tuple-element.322), channel_id=1, source_target_pairs={{0,8},{8,16},{16,24},{24,32},{32,40},{40,48},{48,56},{56,64},{64,7... | collective-permute-start | bytes 491528 | tf_op jit(solution)/shard_map/ppermute | solution.py:17
  75.1 3.7 collective-permute-start.7
  85.2 9.3 %multiply_add_fusion.6 = f32[32,5,16,128]{3,0,2,1:T(8,128)S(1)} fusion(f32[32,5,16,128]{3,0,2,1:T(8,128)} %get-tuple-element.276, f32[32,5,16,128]{3,0,2,1:T(8,128)} %copy-done.2, f32[32,5,20,2]{3,0,2,1:T(8,128)} %copy.241, f32[32,5,2,128]{3,0,2,1:T(8,128)} %copy-done.7, f32[32,5,2,128]{3,0,2,1:T(8,128)} %copy-done.11, f32[32,5,20,2]{3,0,2,1:T(8,128)} %copy.243, ...), kind=kLoop, calls=%fused_computation.116 | loop fusion | flops 17039360 | bytes 7153684 | tf_op jit(solution)/shard_map/add | solution.py:91
  95.8 5.2 %collective-permute-start.9 = (f32[32,5,2,128]{3,0,2,1:T(8,128)S(1)}, f32[32,5,2,128]{3,0,2,1:T(8,128)S(1)}, u32[]{:S(2)}, u32[]{:S(2)}) collective-permute-start(f32[32,5,2,128]{3,0,2,1:T(8,128)S(1)} %get-tuple-element.310), channel_id=1, source_target_pairs={{0,8},{8,16},{16,24},{24,32},{32,40},{40,48},{48,56},{56,64},{64,7... | collective-permute-start | bytes 491528 | tf_op jit(solution)/shard_map/ppermute | solution.py:17
  121.5 5.9 %multiply_add_fusion.4 = (f32[32,5,16,128]{3,0,2,1:T(8,128)S(1)}, f32[32,5,16,128]{3,0,2,1:T(8,128)}) fusion(f32[32,5,16,128]{3,0,2,1:T(8,128)S(1)} %multiply_add_fusion.6, f32[32,16,128]{2,0,1:T(8,128)} %get-tuple-element.316, f32[5,16,128]{2,1,0:T(8,128)S(1)} %get-tuple-element.336, f32[32,16,128]{2,0,1:T(8,128)S(1)} %get-tuple-element.313, ...), kind=kLoop, calls=%fused_computation.114 | loop fusion | flops 16711680 | bytes 5842964 | tf_op jit(solution)/shard_map/add | solution.py:89
  128.7 5.0 %collective-permute-start.13 = (f32[32,5,2,128]{3,0,2,1:T(8,128)S(1)}, f32[32,5,2,128]{3,0,2,1:T(8,128)S(1)}, u32[]{:S(2)}, u32[]{:S(2)}) collective-permute-start(f32[32,5,2,128]{3,0,2,1:T(8,128)S(1)} %get-tuple-element.308), channel_id=1, source_target_pairs={{0,8},{8,16},{16,24},{24,32},{32,40},{40,48},{48,56},{56,64},{64,7... | collective-permute-start | bytes 491528 | tf_op jit(solution)/shard_map/ppermute | solution.py:17
  147.4 3.7 collective-permute-start.15
  157.5 9.2 %multiply_add_fusion.3 = f32[32,5,16,128]{3,0,2,1:T(8,128)S(1)} fusion(f32[32,5,16,128]{3,0,2,1:T(8,128)S(1)} %multiply_add_fusion.6, f32[32,5,16,128]{3,0,2,1:T(8,128)} %get-tuple-element.274, f32[32,5,16,128]{3,0,2,1:T(8,128)} %copy-done.3, f32[32,5,20,2]{3,0,2,1:T(8,128)} %copy.250, f32[32,5,2,128]{3,0,2,1:T(8,128)} %copy-done.6, ...), kind=kLoop, calls=%fused_computation.113 | loop fusion | flops 17039360 | bytes 7153684 | tf_op jit(solution)/shard_map/add | solution.py:91
  168.1 5.0 %collective-permute-start.17 = (f32[32,5,2,128]{3,0,2,1:T(8,128)S(1)}, f32[32,5,2,128]{3,0,2,1:T(8,128)S(1)}, u32[]{:S(2)}, u32[]{:S(2)}) collective-permute-start(f32[32,5,2,128]{3,0,2,1:T(8,128)S(1)} %get-tuple-element.296), channel_id=1, source_target_pairs={{0,8},{8,16},{16,24},{24,32},{32,40},{40,48},{48,56},{56,64},{64,7... | collective-permute-start | bytes 491528 | tf_op jit(solution)/shard_map/ppermute | solution.py:17
  185.1 3.2 collective-permute-start.19
  193.9 5.9 %multiply_add_fusion.1 = (f32[32,5,16,128]{3,0,2,1:T(8,128)S(1)}, f32[32,5,16,128]{3,0,2,1:T(8,128)}) fusion(f32[32,5,16,128]{3,0,2,1:T(8,128)S(1)} %multiply_add_fusion.3, f32[32,16,128]{2,0,1:T(8,128)} %get-tuple-element.302, f32[5,16,128]{2,1,0:T(8,128)S(1)} %get-tuple-element.336, f32[32,16,128]{2,0,1:T(8,128)S(1)} %get-tuple-element.299, ...), kind=kLoop, calls=%fused_computation.111 | loop fusion | flops 16711680 | bytes 5842964 | tf_op jit(solution)/shard_map/add | solution.py:89
  201.7 6.8 %collective-permute-start.21 = (f32[32,5,2,128]{3,0,2,1:T(8,128)S(1)}, f32[32,5,2,128]{3,0,2,1:T(8,128)S(1)}, u32[]{:S(2)}, u32[]{:S(2)}) collective-permute-start(f32[32,5,2,128]{3,0,2,1:T(8,128)S(1)} %get-tuple-element.294), channel_id=1, source_target_pairs={{0,8},{8,16},{16,24},{24,32},{32,40},{40,48},{48,56},{56,64},{64,7... | collective-permute-start | bytes 491528 | tf_op jit(solution)/shard_map/ppermute | solution.py:17
  222.0 3.7 collective-permute-start.23
  232.1 5.3 %multiply_add_fusion = f32[32,5,16,128]{3,0,2,1:T(8,128)S(1)} fusion(f32[32,5,16,128]{3,0,2,1:T(8,128)S(1)} %multiply_add_fusion.3, f32[32,5,16,128]{3,0,2,1:T(8,128)} %get-tuple-element.272, f32[32,5,16,128]{3,0,2,1:T(8,128)S(1)} %get-tuple-element.271, f32[32,5,20,2]{3,0,2,1:T(8,128)} %copy.258, f32[32,5,2,128]{3,0,2,1:T(8,128)} %copy-done.4, ...), kind=kLoop, calls=%fused_computation.110 | loop fusion | flops 17039360 | bytes 7153684 | tf_op jit(solution)/shard_map/add | solution.py:91
  239.3 24.5 %psum.7 = f32[32,32]{0,1:T(8,128)S(1)} all-reduce(f32[32,32]{0,1:T(8,128)S(1)} %fusion.18), channel_id=1, replica_groups=mesh['ax'=16,'rad'=8] {'rad'}, use_global_device_ids=true, to_apply=%region_0.0 | all-reduce | flops 1024 | bytes 8192 | tf_op jit(solution)/shard_map/psum | solution.py:95
  268.3 36.5 %all-gather = f32[512,32]{1,0:T(8,128)S(1)} all-gather(f32[32,32]{1,0:T(8,128)S(1)} %copy.263), channel_id=2, replica_groups=mesh['ax'=16,'rad'=8] {'ax'}, dimensions={0}, use_global_device_ids=true | all-gather | bytes 69632 | tf_op jit(solution)/shard_map/all_gather | solution.py:24
  304.8 70.9 %while.30 = (s32[]{:T(128)}, f32[32,32]{0,1:T(8,128)S(1)}, f32[16,32,32]{2,1,0:T(8,128)S(1)}, s32[]{:T(128)}, s32[]{:T(128)}, /*index=5*/s32[]{:T(128)}) while((s32[]{:T(128)}, f32[32,32]{0,1:T(8,128)S(1)}, f32[16,32,32]{2,1,0:T(8,128)S(1)}, s32[]{:T(128)}, s32[]{:T(128)}, /*index=5*/s32[]{:T(128)}) %tuple.141), condition=%wide.region_4.6_spmd, body=%wide.region_3.5_spmd.sunk | while | flops 795684 | bytes 78197 | solution.py:30
  375.9 90.0 %while.31 = (s32[]{:T(128)}, f32[32,32]{1,0:T(8,128)S(1)}, f32[32,32]{1,0:T(8,128)}, f32[32,32]{1,0:T(8,128)S(1)}, s32[]{:T(128)}, /*index=5*/s32[]{:T(128)}, s32[]{:T(128)}, s32[]{:T(128)}) while((s32[]{:T(128)}, f32[32,32]{1,0:T(8,128)S(1)}, f32[32,32]{1,0:T(8,128)}, f32[32,32]{1,0:T(8,128)S(1)}, s32[]{:T(128)}, /*index=5*/s32[]{:T(128)}, ...), condition=%wide.region_7.9_spmd, body=%wide.region_5.8_spmd.sunk | while | flops 12421 | bytes 18835 | solution.py:70
  (379 shorter events, 298.6 us)
Async XLA Ops:
  2.8 14.4 %collective-permute-start.1 = (f32[32,5,2,128]{3,0,2,1:T(8,128)}, f32[32,5,2,128]{3,0,2,1:T(8,128)}, u32[]{:S(2)}, u32[]{:S(2)}) collective-permute-start(f32[32,5,2,128]{3,0,2,1:T(8,128)} %copy.298), channel_id=1, source_target_pairs={{0,8},{8,16},{16,24},{24,32},{32,40},{40,48},{48,56},{56,64},{64,7... | collective-permute-start | bytes 491528 | tf_op jit(solution)/shard_map/ppermute | solution.py:17
  8.1 10.4 %collective-permute-start = (f32[32,5,2,128]{3,0,2,1:T(8,128)}, f32[32,5,2,128]{3,0,2,1:T(8,128)}, u32[]{:S(2)}, u32[]{:S(2)}) collective-permute-start(f32[32,5,2,128]{3,0,2,1:T(8,128)} %copy.297), channel_id=1, source_target_pairs={{8,0},{16,8},{24,16},{32,24},{40,32},{48,40},{56,48},{64,56},{72,6... | collective-permute-start | bytes 491528 | tf_op jit(solution)/shard_map/ppermute | solution.py:18
  26.3 16.1 %collective-permute-start.2 = (f32[32,5,20,2]{0,2,3,1:T(8,128)S(1)}, f32[32,5,20,2]{0,2,3,1:T(8,128)S(1)}, u32[]{:S(2)}, u32[]{:S(2)}) collective-permute-start(f32[32,5,20,2]{0,2,3,1:T(8,128)S(1)} %get-tuple-element.277), channel_id=1, source_target_pairs={{1,0},{2,1},{3,2},{4,3},{5,4},{6,5},{7,6},{9,8},{10,9},{11,10},{12... | collective-permute-start | bytes 76808 | tf_op jit(solution)/shard_map/ppermute | solution.py:18
  27.6 16.7 %collective-permute-start.3 = (f32[32,5,20,2]{0,2,3,1:T(8,128)S(1)}, f32[32,5,20,2]{0,2,3,1:T(8,128)S(1)}, u32[]{:S(2)}, u32[]{:S(2)}) collective-permute-start(f32[32,5,20,2]{0,2,3,1:T(8,128)S(1)} %get-tuple-element.278), channel_id=1, source_target_pairs={{0,1},{1,2},{2,3},{3,4},{4,5},{5,6},{6,7},{8,9},{9,10},{10,11},{11... | collective-permute-start | bytes 76808 | tf_op jit(solution)/shard_map/ppermute | solution.py:17
  55.0 9.2 %collective-permute-start.4 = (f32[32,5,2,128]{3,0,2,1:T(8,128)S(1)}, f32[32,5,2,128]{3,0,2,1:T(8,128)S(1)}, u32[]{:S(2)}, u32[]{:S(2)}) collective-permute-start(f32[32,5,2,128]{3,0,2,1:T(8,128)S(1)} %get-tuple-element.323), channel_id=1, source_target_pairs={{8,0},{16,8},{24,16},{32,24},{40,32},{48,40},{56,48},{64,56},{72,6... | collective-permute-start | bytes 491528 | tf_op jit(solution)/shard_map/ppermute | solution.py:18
  56.3 9.5 %collective-permute-start.5 = (f32[32,5,2,128]{3,0,2,1:T(8,128)S(1)}, f32[32,5,2,128]{3,0,2,1:T(8,128)S(1)}, u32[]{:S(2)}, u32[]{:S(2)}) collective-permute-start(f32[32,5,2,128]{3,0,2,1:T(8,128)S(1)} %get-tuple-element.322), channel_id=1, source_target_pairs={{0,8},{8,16},{16,24},{24,32},{32,40},{40,48},{48,56},{56,64},{64,7... | collective-permute-start | bytes 491528 | tf_op jit(solution)/shard_map/ppermute | solution.py:17
  70.9 8.8 %collective-permute-start.6 = (f32[32,5,20,2]{0,2,3,1:T(8,128)S(1)}, f32[32,5,20,2]{0,2,3,1:T(8,128)}, u32[]{:S(2)}, u32[]{:S(2)}) collective-permute-start(f32[32,5,20,2]{0,2,3,1:T(8,128)S(1)} %copy.277), channel_id=1, source_target_pairs={{1,0},{2,1},{3,2},{4,3},{5,4},{6,5},{7,6},{9,8},{10,9},{11,10},{12... | collective-permute-start | bytes 76808 | tf_op jit(solution)/shard_map/ppermute | solution.py:18
  75.1 7.4 %collective-permute-start.7 = (f32[32,5,20,2]{0,2,3,1:T(8,128)}, f32[32,5,20,2]{0,2,3,1:T(8,128)}, u32[]{:S(2)}, u32[]{:S(2)}) collective-permute-start(f32[32,5,20,2]{0,2,3,1:T(8,128)} %copy.278), channel_id=1, source_target_pairs={{0,1},{1,2},{2,3},{3,4},{4,5},{5,6},{6,7},{8,9},{9,10},{10,11},{11... | collective-permute-start | bytes 76808 | tf_op jit(solution)/shard_map/ppermute | solution.py:17
  94.5 9.4 %collective-permute-start.8 = (f32[32,5,2,128]{3,0,2,1:T(8,128)S(1)}, f32[32,5,2,128]{3,0,2,1:T(8,128)S(1)}, u32[]{:S(2)}, u32[]{:S(2)}) collective-permute-start(f32[32,5,2,128]{3,0,2,1:T(8,128)S(1)} %get-tuple-element.311), channel_id=1, source_target_pairs={{8,0},{16,8},{24,16},{32,24},{40,32},{48,40},{56,48},{64,56},{72,6... | collective-permute-start | bytes 491528 | tf_op jit(solution)/shard_map/ppermute | solution.py:18
  95.8 9.3 %collective-permute-start.9 = (f32[32,5,2,128]{3,0,2,1:T(8,128)S(1)}, f32[32,5,2,128]{3,0,2,1:T(8,128)S(1)}, u32[]{:S(2)}, u32[]{:S(2)}) collective-permute-start(f32[32,5,2,128]{3,0,2,1:T(8,128)S(1)} %get-tuple-element.310), channel_id=1, source_target_pairs={{0,8},{8,16},{16,24},{24,32},{32,40},{40,48},{48,56},{56,64},{64,7... | collective-permute-start | bytes 491528 | tf_op jit(solution)/shard_map/ppermute | solution.py:17
  110.4 7.5 %collective-permute-start.10 = (f32[32,5,20,2]{0,2,3,1:T(8,128)S(1)}, f32[32,5,20,2]{0,2,3,1:T(8,128)S(1)}, u32[]{:S(2)}, u32[]{:S(2)}) collective-permute-start(f32[32,5,20,2]{0,2,3,1:T(8,128)S(1)} %copy.279), channel_id=1, source_target_pairs={{1,0},{2,1},{3,2},{4,3},{5,4},{6,5},{7,6},{9,8},{10,9},{11,10},{12... | collective-permute-start | bytes 76808 | tf_op jit(solution)/shard_map/ppermute | solution.py:18
  113.9 5.8 %collective-permute-start.11 = (f32[32,5,20,2]{0,2,3,1:T(8,128)S(1)}, f32[32,5,20,2]{0,2,3,1:T(8,128)S(1)}, u32[]{:S(2)}, u32[]{:S(2)}) collective-permute-start(f32[32,5,20,2]{0,2,3,1:T(8,128)S(1)} %copy.280), channel_id=1, source_target_pairs={{0,1},{1,2},{2,3},{3,4},{4,5},{5,6},{6,7},{8,9},{9,10},{10,11},{11... | collective-permute-start | bytes 76808 | tf_op jit(solution)/shard_map/ppermute | solution.py:17
  127.4 9.0 %collective-permute-start.12 = (f32[32,5,2,128]{3,0,2,1:T(8,128)S(1)}, f32[32,5,2,128]{3,0,2,1:T(8,128)S(1)}, u32[]{:S(2)}, u32[]{:S(2)}) collective-permute-start(f32[32,5,2,128]{3,0,2,1:T(8,128)S(1)} %get-tuple-element.309), channel_id=1, source_target_pairs={{8,0},{16,8},{24,16},{32,24},{40,32},{48,40},{56,48},{64,56},{72,6... | collective-permute-start | bytes 491528 | tf_op jit(solution)/shard_map/ppermute | solution.py:18
  128.7 9.4 %collective-permute-start.13 = (f32[32,5,2,128]{3,0,2,1:T(8,128)S(1)}, f32[32,5,2,128]{3,0,2,1:T(8,128)S(1)}, u32[]{:S(2)}, u32[]{:S(2)}) collective-permute-start(f32[32,5,2,128]{3,0,2,1:T(8,128)S(1)} %get-tuple-element.308), channel_id=1, source_target_pairs={{0,8},{8,16},{16,24},{24,32},{32,40},{40,48},{48,56},{56,64},{64,7... | collective-permute-start | bytes 491528 | tf_op jit(solution)/shard_map/ppermute | solution.py:17
  143.2 8.8 %collective-permute-start.14 = (f32[32,5,20,2]{0,2,3,1:T(8,128)S(1)}, f32[32,5,20,2]{0,2,3,1:T(8,128)}, u32[]{:S(2)}, u32[]{:S(2)}) collective-permute-start(f32[32,5,20,2]{0,2,3,1:T(8,128)S(1)} %copy.281), channel_id=1, source_target_pairs={{1,0},{2,1},{3,2},{4,3},{5,4},{6,5},{7,6},{9,8},{10,9},{11,10},{12... | collective-permute-start | bytes 76808 | tf_op jit(solution)/shard_map/ppermute | solution.py:18
  147.4 7.4 %collective-permute-start.15 = (f32[32,5,20,2]{0,2,3,1:T(8,128)}, f32[32,5,20,2]{0,2,3,1:T(8,128)}, u32[]{:S(2)}, u32[]{:S(2)}) collective-permute-start(f32[32,5,20,2]{0,2,3,1:T(8,128)} %copy.282), channel_id=1, source_target_pairs={{0,1},{1,2},{2,3},{3,4},{4,5},{5,6},{6,7},{8,9},{9,10},{10,11},{11... | collective-permute-start | bytes 76808 | tf_op jit(solution)/shard_map/ppermute | solution.py:17
  166.8 9.1 %collective-permute-start.16 = (f32[32,5,2,128]{3,0,2,1:T(8,128)S(1)}, f32[32,5,2,128]{3,0,2,1:T(8,128)S(1)}, u32[]{:S(2)}, u32[]{:S(2)}) collective-permute-start(f32[32,5,2,128]{3,0,2,1:T(8,128)S(1)} %get-tuple-element.297), channel_id=1, source_target_pairs={{8,0},{16,8},{24,16},{32,24},{40,32},{48,40},{56,48},{64,56},{72,6... | collective-permute-start | bytes 491528 | tf_op jit(solution)/shard_map/ppermute | solution.py:18
  168.1 9.5 %collective-permute-start.17 = (f32[32,5,2,128]{3,0,2,1:T(8,128)S(1)}, f32[32,5,2,128]{3,0,2,1:T(8,128)S(1)}, u32[]{:S(2)}, u32[]{:S(2)}) collective-permute-start(f32[32,5,2,128]{3,0,2,1:T(8,128)S(1)} %get-tuple-element.296), channel_id=1, source_target_pairs={{0,8},{8,16},{16,24},{24,32},{32,40},{40,48},{48,56},{56,64},{64,7... | collective-permute-start | bytes 491528 | tf_op jit(solution)/shard_map/ppermute | solution.py:17
  182.4 6.9 %collective-permute-start.18 = (f32[32,5,20,2]{0,2,3,1:T(8,128)S(1)}, f32[32,5,20,2]{0,2,3,1:T(8,128)}, u32[]{:S(2)}, u32[]{:S(2)}) collective-permute-start(f32[32,5,20,2]{0,2,3,1:T(8,128)S(1)} %copy.283), channel_id=1, source_target_pairs={{1,0},{2,1},{3,2},{4,3},{5,4},{6,5},{7,6},{9,8},{10,9},{11,10},{12... | collective-permute-start | bytes 76808 | tf_op jit(solution)/shard_map/ppermute | solution.py:18
  185.1 6.9 %collective-permute-start.19 = (f32[32,5,20,2]{0,2,3,1:T(8,128)}, f32[32,5,20,2]{0,2,3,1:T(8,128)S(1)}, u32[]{:S(2)}, u32[]{:S(2)}) collective-permute-start(f32[32,5,20,2]{0,2,3,1:T(8,128)} %copy.284), channel_id=1, source_target_pairs={{0,1},{1,2},{2,3},{3,4},{4,5},{5,6},{6,7},{8,9},{9,10},{10,11},{11... | collective-permute-start | bytes 76808 | tf_op jit(solution)/shard_map/ppermute | solution.py:17
  200.4 10.7 %collective-permute-start.20 = (f32[32,5,2,128]{3,0,2,1:T(8,128)}, f32[32,5,2,128]{3,0,2,1:T(8,128)S(1)}, u32[]{:S(2)}, u32[]{:S(2)}) collective-permute-start(f32[32,5,2,128]{3,0,2,1:T(8,128)} %get-tuple-element.295), channel_id=1, source_target_pairs={{8,0},{16,8},{24,16},{32,24},{40,32},{48,40},{56,48},{64,56},{72,6... | collective-permute-start | bytes 491528 | tf_op jit(solution)/shard_map/ppermute | solution.py:18
  201.7 11.0 %collective-permute-start.21 = (f32[32,5,2,128]{3,0,2,1:T(8,128)S(1)}, f32[32,5,2,128]{3,0,2,1:T(8,128)S(1)}, u32[]{:S(2)}, u32[]{:S(2)}) collective-permute-start(f32[32,5,2,128]{3,0,2,1:T(8,128)S(1)} %get-tuple-element.294), channel_id=1, source_target_pairs={{0,8},{8,16},{16,24},{24,32},{32,40},{40,48},{48,56},{56,64},{64,7... | collective-permute-start | bytes 491528 | tf_op jit(solution)/shard_map/ppermute | solution.py:17
  217.9 8.7 %collective-permute-start.22 = (f32[32,5,20,2]{0,2,3,1:T(8,128)S(1)}, f32[32,5,20,2]{0,2,3,1:T(8,128)}, u32[]{:S(2)}, u32[]{:S(2)}) collective-permute-start(f32[32,5,20,2]{0,2,3,1:T(8,128)S(1)} %copy.285), channel_id=1, source_target_pairs={{1,0},{2,1},{3,2},{4,3},{5,4},{6,5},{7,6},{9,8},{10,9},{11,10},{12... | collective-permute-start | bytes 76808 | tf_op jit(solution)/shard_map/ppermute | solution.py:18
  222.0 7.4 %collective-permute-start.23 = (f32[32,5,20,2]{0,2,3,1:T(8,128)}, f32[32,5,20,2]{0,2,3,1:T(8,128)}, u32[]{:S(2)}, u32[]{:S(2)}) collective-permute-start(f32[32,5,20,2]{0,2,3,1:T(8,128)} %copy.286), channel_id=1, source_target_pairs={{0,1},{1,2},{2,3},{3,4},{4,5},{5,6},{6,7},{8,9},{9,10},{10,11},{11... | collective-permute-start | bytes 76808 | tf_op jit(solution)/shard_map/ppermute | solution.py:17
  (24 other events, 119.2 us)
where the time goes:
time: 474 us; the launch traced here: 470 us
  other arithmetic  159 us (34%)
  local copies, waits for them, and re-layouts  104 us (22%)
  starting transfers between devices  67.7 us (14%)
  blocking collectives  61 us (13%)
  matrix products  54.9 us (12%)
  waiting for transfers between devices  20.9 us (4%)
    another operation x45, other arithmetic, join_factors(): return jnp.linalg.cholesky(summed).T  53.9 us
    ppermute x12, starting transfers between devices, padded_2(): before = lax.ppermute(last, axis, up)  52.2 us
    dot_general x32, matrix products, one_row(): jnp.dot(factor_row, inverse, precision=lax.Precision.HIGHEST)  46.9 us
    unnamed x66, local copies, waits for them, and re-layouts  41.9 us
    reduce_sum x32, other arithmetic, one_row(): pivot = jnp.sum(factor_row * unit_row)  41.6 us
    all_gather x1, blocking collectives, combined_all(): everything = lax.all_gather(shard, axis)  36.5 us
    psum x1, blocking collectives, per_device(): radial_gram = lax.psum(local_gram, 'rad')  24.5 us
    add x3, other arithmetic, per_device(): field_now = field_now + 0.5 * time_step * (slope_one + slope_two)  23.8 us
  transfers between devices with their start and end apart: 24, of which 10 were waited for; matrix products, arithmetic and copies ran while one was open for 11% of the time, Pallas kernels for 0%

commit v1 on v0

--- a/solution.py
+++ b/solution.py
@@ -92,7 +92,11 @@
     flattened = field_now.reshape(vectors, variables * axial_cells * radial_cells)
     rows_all = variables * axial_cells * radial_cells * lax.axis_size("ax") * lax.axis_size("rad")
     local_gram = jnp.dot(flattened, flattened.T, precision=lax.Precision.HIGHEST) / rows_all
-    radial_gram = lax.psum(local_gram, "rad")
+    radial_gram = local_gram
+    for hop in (1, 2, 4):
+        radial_gram = radial_gram + lax.ppermute(
+            radial_gram, "rad", [(dev, dev ^ hop) for dev in range(8)]
+        )
     start_factor = jnp.linalg.cholesky(radial_gram).T
     upper_factor = combined_all(start_factor, "ax", join_factors)
     inverse = upper_inverse(upper_factor)

time: 474 us -> 412 us (0.87)
  blocking collectives: 61 us -> 36.5 us
  other arithmetic: 159 us -> 136 us
  matrix products: 54.9 us -> 33 us
  waiting for transfers between devices: 20.9 us -> 26.9 us
    psum x1 -> x0, blocking collectives: 24.5 us -> none  [per_device(): radial_gram = lax.psum(local_gram, 'rad')]
    reduce_sum x32, other arithmetic: 41.6 us -> 19.5 us  [one_row(): pivot = jnp.sum(factor_row * unit_row)]
    dot_general x32, matrix products: 46.9 us -> 24.9 us  [one_row(): jnp.dot(factor_row, inverse, precision=lax.Precision.HIGHEST)]
    ppermute x0 -> x3, waiting for transfers between devices: none -> 5.42 us  [per_device(): lax.ppermute(radial_gram, 'rad', [(dev, dev ^ hop) for dev in range(8)])]
    unnamed x66 -> x68, local copies, waits for them, and re-layouts: 41.9 us -> 41.6 us
  transfers between devices with their start and end apart: 24 -> 27, of which waited for: 10 -> 13; matrix products, arithmetic and copies ran while one was open for 11% -> 13% of each run, Pallas kernels for 0% -> 0%
where the time goes in v1:
time: 412 us; the launch traced here: 410 us
  other arithmetic  136 us (33%)
  local copies, waits for them, and re-layouts  105 us (25%)
  starting transfers between devices  70.6 us (17%)
  blocking collectives  36.5 us (9%)
  matrix products  33 us (8%)
  waiting for transfers between devices  26.9 us (7%)
    another operation x45, other arithmetic, join_factors(): return jnp.linalg.cholesky(summed).T  53.9 us
    ppermute x12, starting transfers between devices, padded_2(): before = lax.ppermute(last, axis, up)  52.2 us
    unnamed x68, local copies, waits for them, and re-layouts  41.6 us
    all_gather x1, blocking collectives, combined_all(): everything = lax.all_gather(shard, axis)  36.5 us
    dot_general x32, matrix products, one_row(): jnp.dot(factor_row, inverse, precision=lax.Precision.HIGHEST)  24.9 us
    add x3, other arithmetic, per_device(): field_now = field_now + 0.5 * time_step * (slope_one + slope_two)  23.8 us
    add x3, other arithmetic, per_device(): middle = field_now + time_step * slope_one  20.3 us
    reduce_sum x32, other arithmetic, one_row(): pivot = jnp.sum(factor_row * unit_row)  19.5 us
  transfers between devices with their start and end apart: 27, of which 13 were waited for; matrix products, arithmetic and copies ran while one was open for 13% of the time, Pallas kernels for 0%

profile of v1, /device:TPU:0, one launch (start us, length us, event | category | flops | bytes accessed | tf_op | source)
XLA Modules:
  0.0 409.8 jit_solution(13626814360584305634)
XLA Ops:
  2.8 4.6 %collective-permute-start.1 = (f32[32,5,2,128]{3,0,2,1:T(8,128)}, f32[32,5,2,128]{3,0,2,1:T(8,128)}, u32[]{:S(2)}, u32[]{:S(2)}) collective-permute-start(f32[32,5,2,128]{3,0,2,1:T(8,128)} %copy.298), channel_id=1, source_target_pairs={{0,8},{8,16},{16,24},{24,32},{32,40},{40,48},{48,56},{56,64},{64,7... | collective-permute-start | bytes 491528 | tf_op jit(solution)/shard_map/ppermute | solution.py:17
  9.4 4.3 %copy.227 = f32[32,5,16,128]{0,2,3,1:T(8,128)} copy(f32[32,5,16,128]{3,2,1,0:T(8,128)S(1)} %copy-done) | data formatting | bytes 2621440 | tf_op args[0]
  19.7 3.5 pad_maximum_fusion
  23.2 3.1 copy-done.1
  36.0 6.5 %copy.229 = f32[32,5,20,128]{3,0,2,1:T(8,128)} copy(f32[32,5,20,128]{0,2,3,1:T(8,128)} %copy-done.1) | data formatting | bytes 3276800 | tf_op jit(solution)/shard_map/concatenate | solution.py:19
  46.2 8.7 %multiply_add_fusion.7 = (f32[32,5,16,128]{3,0,2,1:T(8,128)S(1)}, f32[32,5,16,128]{3,0,2,1:T(8,128)}) fusion(f32[32,5,16,128]{3,2,1,0:T(8,128)S(1)} %copy-done, f32[32,16,128]{2,0,1:T(8,128)} %copy.238, f32[5,16,128]{2,1,0:T(8,128)S(1)} %get-tuple-element.336, f32[32,16,128]{2,0,1:T(8,128)} %copy.237, f32[5,16,128]{2,1,0:T(8,128)S(1)} %get-tuple-element.337, ...), kind=kLoop, calls=%fused_computation.117 | loop fusion | flops 12779520 | bytes 12396564 | tf_op jit(solution)/shard_map/add | solution.py:89
  56.2 5.2 %collective-permute-start.5 = (f32[32,5,2,128]{3,0,2,1:T(8,128)S(1)}, f32[32,5,2,128]{3,0,2,1:T(8,128)S(1)}, u32[]{:S(2)}, u32[]{:S(2)}) collective-permute-start(f32[32,5,2,128]{3,0,2,1:T(8,128)S(1)} %get-tuple-element.322), channel_id=1, source_target_pairs={{0,8},{8,16},{16,24},{24,32},{32,40},{40,48},{48,56},{56,64},{64,7... | collective-permute-start | bytes 491528 | tf_op jit(solution)/shard_map/ppermute | solution.py:17
  75.0 3.7 collective-permute-start.7
  85.1 9.4 %multiply_add_fusion.6 = f32[32,5,16,128]{3,0,2,1:T(8,128)S(1)} fusion(f32[32,5,16,128]{3,0,2,1:T(8,128)} %get-tuple-element.276, f32[32,5,16,128]{3,0,2,1:T(8,128)} %copy-done.2, f32[32,5,20,2]{3,0,2,1:T(8,128)} %copy.241, f32[32,5,2,128]{3,0,2,1:T(8,128)} %copy-done.8, f32[32,5,2,128]{3,0,2,1:T(8,128)} %copy-done.12, f32[32,5,20,2]{3,0,2,1:T(8,128)} %copy.243, ...), kind=kLoop, calls=%fused_computation.116 | loop fusion | flops 17039360 | bytes 7153684 | tf_op jit(solution)/shard_map/add | solution.py:91
  95.8 5.2 %collective-permute-start.9 = (f32[32,5,2,128]{3,0,2,1:T(8,128)S(1)}, f32[32,5,2,128]{3,0,2,1:T(8,128)S(1)}, u32[]{:S(2)}, u32[]{:S(2)}) collective-permute-start(f32[32,5,2,128]{3,0,2,1:T(8,128)S(1)} %get-tuple-element.310), channel_id=1, source_target_pairs={{0,8},{8,16},{16,24},{24,32},{32,40},{40,48},{48,56},{56,64},{64,7... | collective-permute-start | bytes 491528 | tf_op jit(solution)/shard_map/ppermute | solution.py:17
  113.8 3.0 collective-permute-start.11
  121.5 5.8 %multiply_add_fusion.4 = (f32[32,5,16,128]{3,0,2,1:T(8,128)S(1)}, f32[32,5,16,128]{3,0,2,1:T(8,128)}) fusion(f32[32,5,16,128]{3,0,2,1:T(8,128)S(1)} %multiply_add_fusion.6, f32[32,16,128]{2,0,1:T(8,128)} %get-tuple-element.316, f32[5,16,128]{2,1,0:T(8,128)S(1)} %get-tuple-element.336, f32[32,16,128]{2,0,1:T(8,128)S(1)} %get-tuple-element.313, ...), kind=kLoop, calls=%fused_computation.114 | loop fusion | flops 16711680 | bytes 5842964 | tf_op jit(solution)/shard_map/add | solution.py:89
  128.6 5.0 %collective-permute-start.13 = (f32[32,5,2,128]{3,0,2,1:T(8,128)S(1)}, f32[32,5,2,128]{3,0,2,1:T(8,128)S(1)}, u32[]{:S(2)}, u32[]{:S(2)}) collective-permute-start(f32[32,5,2,128]{3,0,2,1:T(8,128)S(1)} %get-tuple-element.308), channel_id=1, source_target_pairs={{0,8},{8,16},{16,24},{24,32},{32,40},{40,48},{48,56},{56,64},{64,7... | collective-permute-start | bytes 491528 | tf_op jit(solution)/shard_map/ppermute | solution.py:17
  147.3 3.7 collective-permute-start.15
  157.3 9.3 %multiply_add_fusion.3 = f32[32,5,16,128]{3,0,2,1:T(8,128)S(1)} fusion(f32[32,5,16,128]{3,0,2,1:T(8,128)S(1)} %multiply_add_fusion.6, f32[32,5,16,128]{3,0,2,1:T(8,128)} %get-tuple-element.274, f32[32,5,16,128]{3,0,2,1:T(8,128)} %copy-done.3, f32[32,5,20,2]{3,0,2,1:T(8,128)} %copy.250, f32[32,5,2,128]{3,0,2,1:T(8,128)} %copy-done.7, ...), kind=kLoop, calls=%fused_computation.113 | loop fusion | flops 17039360 | bytes 7153684 | tf_op jit(solution)/shard_map/add | solution.py:91
  168.0 5.0 %collective-permute-start.17 = (f32[32,5,2,128]{3,0,2,1:T(8,128)S(1)}, f32[32,5,2,128]{3,0,2,1:T(8,128)S(1)}, u32[]{:S(2)}, u32[]{:S(2)}) collective-permute-start(f32[32,5,2,128]{3,0,2,1:T(8,128)S(1)} %get-tuple-element.296), channel_id=1, source_target_pairs={{0,8},{8,16},{16,24},{24,32},{32,40},{40,48},{48,56},{56,64},{64,7... | collective-permute-start | bytes 491528 | tf_op jit(solution)/shard_map/ppermute | solution.py:17
  185.0 3.2 collective-permute-start.19
  193.8 5.8 %multiply_add_fusion.1 = (f32[32,5,16,128]{3,0,2,1:T(8,128)S(1)}, f32[32,5,16,128]{3,0,2,1:T(8,128)}) fusion(f32[32,5,16,128]{3,0,2,1:T(8,128)S(1)} %multiply_add_fusion.3, f32[32,16,128]{2,0,1:T(8,128)} %get-tuple-element.302, f32[5,16,128]{2,1,0:T(8,128)S(1)} %get-tuple-element.336, f32[32,16,128]{2,0,1:T(8,128)S(1)} %get-tuple-element.299, ...), kind=kLoop, calls=%fused_computation.111 | loop fusion | flops 16711680 | bytes 5842964 | tf_op jit(solution)/shard_map/add | solution.py:89
  200.9 6.9 %collective-permute-start.21 = (f32[32,5,2,128]{3,0,2,1:T(8,128)S(1)}, f32[32,5,2,128]{3,0,2,1:T(8,128)S(1)}, u32[]{:S(2)}, u32[]{:S(2)}) collective-permute-start(f32[32,5,2,128]{3,0,2,1:T(8,128)S(1)} %get-tuple-element.294), channel_id=1, source_target_pairs={{0,8},{8,16},{16,24},{24,32},{32,40},{40,48},{48,56},{56,64},{64,7... | collective-permute-start | bytes 491528 | tf_op jit(solution)/shard_map/ppermute | solution.py:17
  221.2 3.7 collective-permute-start.23
  231.3 5.1 %multiply_add_fusion = f32[32,5,16,128]{3,0,2,1:T(8,128)S(1)} fusion(f32[32,5,16,128]{3,0,2,1:T(8,128)S(1)} %multiply_add_fusion.3, f32[32,5,16,128]{3,0,2,1:T(8,128)} %get-tuple-element.272, f32[32,5,16,128]{3,0,2,1:T(8,128)S(1)} %get-tuple-element.271, f32[32,5,20,2]{3,0,2,1:T(8,128)} %copy.258, f32[32,5,2,128]{3,0,2,1:T(8,128)} %copy-done.5, ...), kind=kLoop, calls=%fused_computation.110 | loop fusion | flops 17039360 | bytes 7153684 | tf_op jit(solution)/shard_map/add | solution.py:91
  253.0 36.5 %all-gather = f32[512,32]{1,0:T(8,128)S(1)} all-gather(f32[32,32]{1,0:T(8,128)S(1)} %copy.263), channel_id=2, replica_groups=mesh['ax'=16,'rad'=8] {'ax'}, dimensions={0}, use_global_device_ids=true | all-gather | bytes 69632 | tf_op jit(solution)/shard_map/all_gather | solution.py:24
  289.6 70.9 %while.30 = (s32[]{:T(128)}, f32[32,32]{0,1:T(8,128)S(1)}, f32[16,32,32]{2,1,0:T(8,128)S(1)}, s32[]{:T(128)}, s32[]{:T(128)}, /*index=5*/s32[]{:T(128)}) while((s32[]{:T(128)}, f32[32,32]{0,1:T(8,128)S(1)}, f32[16,32,32]{2,1,0:T(8,128)S(1)}, s32[]{:T(128)}, s32[]{:T(128)}, /*index=5*/s32[]{:T(128)}) %tuple.141), condition=%wide.region_3.5_spmd, body=%wide.region_2.4_spmd.sunk | while | flops 795684 | bytes 78197 | solution.py:30
  360.6 45.8 %while.31 = (s32[]{:T(128)}, f32[32,32]{1,0:T(8,128)S(1)}, f32[32,32]{1,0:T(8,128)S(1)}, f32[32,32]{1,0:T(8,128)S(1)}, s32[]{:T(128)}, /*index=5*/s32[]{:T(128)}, s32[]{:T(128)}, s32[]{:T(128)}) while((s32[]{:T(128)}, f32[32,32]{1,0:T(8,128)S(1)}, f32[32,32]{1,0:T(8,128)S(1)}, f32[32,32]{1,0:T(8,128)S(1)}, s32[]{:T(128)}, ...), condition=%wide.region_6.8_spmd, body=%wide.region_4.7_spmd.sunk | while | flops 12421 | bytes 19219 | solution.py:70
  (389 shorter events, 260.1 us)
Async XLA Ops:
  2.8 14.4 %collective-permute-start.1 = (f32[32,5,2,128]{3,0,2,1:T(8,128)}, f32[32,5,2,128]{3,0,2,1:T(8,128)}, u32[]{:S(2)}, u32[]{:S(2)}) collective-permute-start(f32[32,5,2,128]{3,0,2,1:T(8,128)} %copy.298), channel_id=1, source_target_pairs={{0,8},{8,16},{16,24},{24,32},{32,40},{40,48},{48,56},{56,64},{64,7... | collective-permute-start | bytes 491528 | tf_op jit(solution)/shard_map/ppermute | solution.py:17
  8.1 10.4 %collective-permute-start = (f32[32,5,2,128]{3,0,2,1:T(8,128)}, f32[32,5,2,128]{3,0,2,1:T(8,128)}, u32[]{:S(2)}, u32[]{:S(2)}) collective-permute-start(f32[32,5,2,128]{3,0,2,1:T(8,128)} %copy.297), channel_id=1, source_target_pairs={{8,0},{16,8},{24,16},{32,24},{40,32},{48,40},{56,48},{64,56},{72,6... | collective-permute-start | bytes 491528 | tf_op jit(solution)/shard_map/ppermute | solution.py:18
  26.4 16.1 %collective-permute-start.2 = (f32[32,5,20,2]{0,2,3,1:T(8,128)S(1)}, f32[32,5,20,2]{0,2,3,1:T(8,128)S(1)}, u32[]{:S(2)}, u32[]{:S(2)}) collective-permute-start(f32[32,5,20,2]{0,2,3,1:T(8,128)S(1)} %get-tuple-element.277), channel_id=1, source_target_pairs={{1,0},{2,1},{3,2},{4,3},{5,4},{6,5},{7,6},{9,8},{10,9},{11,10},{12... | collective-permute-start | bytes 76808 | tf_op jit(solution)/shard_map/ppermute | solution.py:18
  27.7 16.6 %collective-permute-start.3 = (f32[32,5,20,2]{0,2,3,1:T(8,128)S(1)}, f32[32,5,20,2]{0,2,3,1:T(8,128)S(1)}, u32[]{:S(2)}, u32[]{:S(2)}) collective-permute-start(f32[32,5,20,2]{0,2,3,1:T(8,128)S(1)} %get-tuple-element.278), channel_id=1, source_target_pairs={{0,1},{1,2},{2,3},{3,4},{4,5},{5,6},{6,7},{8,9},{9,10},{10,11},{11... | collective-permute-start | bytes 76808 | tf_op jit(solution)/shard_map/ppermute | solution.py:17
  54.9 9.2 %collective-permute-start.4 = (f32[32,5,2,128]{3,0,2,1:T(8,128)S(1)}, f32[32,5,2,128]{3,0,2,1:T(8,128)S(1)}, u32[]{:S(2)}, u32[]{:S(2)}) collective-permute-start(f32[32,5,2,128]{3,0,2,1:T(8,128)S(1)} %get-tuple-element.323), channel_id=1, source_target_pairs={{8,0},{16,8},{24,16},{32,24},{40,32},{48,40},{56,48},{64,56},{72,6... | collective-permute-start | bytes 491528 | tf_op jit(solution)/shard_map/ppermute | solution.py:18
  56.2 9.5 %collective-permute-start.5 = (f32[32,5,2,128]{3,0,2,1:T(8,128)S(1)}, f32[32,5,2,128]{3,0,2,1:T(8,128)S(1)}, u32[]{:S(2)}, u32[]{:S(2)}) collective-permute-start(f32[32,5,2,128]{3,0,2,1:T(8,128)S(1)} %get-tuple-element.322), channel_id=1, source_target_pairs={{0,8},{8,16},{16,24},{24,32},{32,40},{40,48},{48,56},{56,64},{64,7... | collective-permute-start | bytes 491528 | tf_op jit(solution)/shard_map/ppermute | solution.py:17
  70.9 8.7 %collective-permute-start.6 = (f32[32,5,20,2]{0,2,3,1:T(8,128)S(1)}, f32[32,5,20,2]{0,2,3,1:T(8,128)}, u32[]{:S(2)}, u32[]{:S(2)}) collective-permute-start(f32[32,5,20,2]{0,2,3,1:T(8,128)S(1)} %copy.277), channel_id=1, source_target_pairs={{1,0},{2,1},{3,2},{4,3},{5,4},{6,5},{7,6},{9,8},{10,9},{11,10},{12... | collective-permute-start | bytes 76808 | tf_op jit(solution)/shard_map/ppermute | solution.py:18
  75.0 7.4 %collective-permute-start.7 = (f32[32,5,20,2]{0,2,3,1:T(8,128)}, f32[32,5,20,2]{0,2,3,1:T(8,128)}, u32[]{:S(2)}, u32[]{:S(2)}) collective-permute-start(f32[32,5,20,2]{0,2,3,1:T(8,128)} %copy.278), channel_id=1, source_target_pairs={{0,1},{1,2},{2,3},{3,4},{4,5},{5,6},{6,7},{8,9},{9,10},{10,11},{11... | collective-permute-start | bytes 76808 | tf_op jit(solution)/shard_map/ppermute | solution.py:17
  94.5 9.4 %collective-permute-start.8 = (f32[32,5,2,128]{3,0,2,1:T(8,128)S(1)}, f32[32,5,2,128]{3,0,2,1:T(8,128)S(1)}, u32[]{:S(2)}, u32[]{:S(2)}) collective-permute-start(f32[32,5,2,128]{3,0,2,1:T(8,128)S(1)} %get-tuple-element.311), channel_id=1, source_target_pairs={{8,0},{16,8},{24,16},{32,24},{40,32},{48,40},{56,48},{64,56},{72,6... | collective-permute-start | bytes 491528 | tf_op jit(solution)/shard_map/ppermute | solution.py:18
  95.8 9.4 %collective-permute-start.9 = (f32[32,5,2,128]{3,0,2,1:T(8,128)S(1)}, f32[32,5,2,128]{3,0,2,1:T(8,128)S(1)}, u32[]{:S(2)}, u32[]{:S(2)}) collective-permute-start(f32[32,5,2,128]{3,0,2,1:T(8,128)S(1)} %get-tuple-element.310), channel_id=1, source_target_pairs={{0,8},{8,16},{16,24},{24,32},{32,40},{40,48},{48,56},{56,64},{64,7... | collective-permute-start | bytes 491528 | tf_op jit(solution)/shard_map/ppermute | solution.py:17
  110.3 7.5 %collective-permute-start.10 = (f32[32,5,20,2]{0,2,3,1:T(8,128)S(1)}, f32[32,5,20,2]{0,2,3,1:T(8,128)S(1)}, u32[]{:S(2)}, u32[]{:S(2)}) collective-permute-start(f32[32,5,20,2]{0,2,3,1:T(8,128)S(1)} %copy.279), channel_id=1, source_target_pairs={{1,0},{2,1},{3,2},{4,3},{5,4},{6,5},{7,6},{9,8},{10,9},{11,10},{12... | collective-permute-start | bytes 76808 | tf_op jit(solution)/shard_map/ppermute | solution.py:18
  113.8 5.8 %collective-permute-start.11 = (f32[32,5,20,2]{0,2,3,1:T(8,128)S(1)}, f32[32,5,20,2]{0,2,3,1:T(8,128)S(1)}, u32[]{:S(2)}, u32[]{:S(2)}) collective-permute-start(f32[32,5,20,2]{0,2,3,1:T(8,128)S(1)} %copy.280), channel_id=1, source_target_pairs={{0,1},{1,2},{2,3},{3,4},{4,5},{5,6},{6,7},{8,9},{9,10},{10,11},{11... | collective-permute-start | bytes 76808 | tf_op jit(solution)/shard_map/ppermute | solution.py:17
  127.3 9.0 %collective-permute-start.12 = (f32[32,5,2,128]{3,0,2,1:T(8,128)S(1)}, f32[32,5,2,128]{3,0,2,1:T(8,128)S(1)}, u32[]{:S(2)}, u32[]{:S(2)}) collective-permute-start(f32[32,5,2,128]{3,0,2,1:T(8,128)S(1)} %get-tuple-element.309), channel_id=1, source_target_pairs={{8,0},{16,8},{24,16},{32,24},{40,32},{48,40},{56,48},{64,56},{72,6... | collective-permute-start | bytes 491528 | tf_op jit(solution)/shard_map/ppermute | solution.py:18
  128.6 9.4 %collective-permute-start.13 = (f32[32,5,2,128]{3,0,2,1:T(8,128)S(1)}, f32[32,5,2,128]{3,0,2,1:T(8,128)S(1)}, u32[]{:S(2)}, u32[]{:S(2)}) collective-permute-start(f32[32,5,2,128]{3,0,2,1:T(8,128)S(1)} %get-tuple-element.308), channel_id=1, source_target_pairs={{0,8},{8,16},{16,24},{24,32},{32,40},{40,48},{48,56},{56,64},{64,7... | collective-permute-start | bytes 491528 | tf_op jit(solution)/shard_map/ppermute | solution.py:17
  143.1 8.7 %collective-permute-start.14 = (f32[32,5,20,2]{0,2,3,1:T(8,128)S(1)}, f32[32,5,20,2]{0,2,3,1:T(8,128)}, u32[]{:S(2)}, u32[]{:S(2)}) collective-permute-start(f32[32,5,20,2]{0,2,3,1:T(8,128)S(1)} %copy.281), channel_id=1, source_target_pairs={{1,0},{2,1},{3,2},{4,3},{5,4},{6,5},{7,6},{9,8},{10,9},{11,10},{12... | collective-permute-start | bytes 76808 | tf_op jit(solution)/shard_map/ppermute | solution.py:18
  147.3 7.4 %collective-permute-start.15 = (f32[32,5,20,2]{0,2,3,1:T(8,128)}, f32[32,5,20,2]{0,2,3,1:T(8,128)}, u32[]{:S(2)}, u32[]{:S(2)}) collective-permute-start(f32[32,5,20,2]{0,2,3,1:T(8,128)} %copy.282), channel_id=1, source_target_pairs={{0,1},{1,2},{2,3},{3,4},{4,5},{5,6},{6,7},{8,9},{9,10},{10,11},{11... | collective-permute-start | bytes 76808 | tf_op jit(solution)/shard_map/ppermute | solution.py:17
  166.7 9.1 %collective-permute-start.16 = (f32[32,5,2,128]{3,0,2,1:T(8,128)S(1)}, f32[32,5,2,128]{3,0,2,1:T(8,128)S(1)}, u32[]{:S(2)}, u32[]{:S(2)}) collective-permute-start(f32[32,5,2,128]{3,0,2,1:T(8,128)S(1)} %get-tuple-element.297), channel_id=1, source_target_pairs={{8,0},{16,8},{24,16},{32,24},{40,32},{48,40},{56,48},{64,56},{72,6... | collective-permute-start | bytes 491528 | tf_op jit(solution)/shard_map/ppermute | solution.py:18
  168.0 9.5 %collective-permute-start.17 = (f32[32,5,2,128]{3,0,2,1:T(8,128)S(1)}, f32[32,5,2,128]{3,0,2,1:T(8,128)S(1)}, u32[]{:S(2)}, u32[]{:S(2)}) collective-permute-start(f32[32,5,2,128]{3,0,2,1:T(8,128)S(1)} %get-tuple-element.296), channel_id=1, source_target_pairs={{0,8},{8,16},{16,24},{24,32},{32,40},{40,48},{48,56},{56,64},{64,7... | collective-permute-start | bytes 491528 | tf_op jit(solution)/shard_map/ppermute | solution.py:17
  182.2 6.9 %collective-permute-start.18 = (f32[32,5,20,2]{0,2,3,1:T(8,128)S(1)}, f32[32,5,20,2]{0,2,3,1:T(8,128)}, u32[]{:S(2)}, u32[]{:S(2)}) collective-permute-start(f32[32,5,20,2]{0,2,3,1:T(8,128)S(1)} %copy.283), channel_id=1, source_target_pairs={{1,0},{2,1},{3,2},{4,3},{5,4},{6,5},{7,6},{9,8},{10,9},{11,10},{12... | collective-permute-start | bytes 76808 | tf_op jit(solution)/shard_map/ppermute | solution.py:18
  185.0 7.0 %collective-permute-start.19 = (f32[32,5,20,2]{0,2,3,1:T(8,128)}, f32[32,5,20,2]{0,2,3,1:T(8,128)S(1)}, u32[]{:S(2)}, u32[]{:S(2)}) collective-permute-start(f32[32,5,20,2]{0,2,3,1:T(8,128)} %copy.284), channel_id=1, source_target_pairs={{0,1},{1,2},{2,3},{3,4},{4,5},{5,6},{6,7},{8,9},{9,10},{10,11},{11... | collective-permute-start | bytes 76808 | tf_op jit(solution)/shard_map/ppermute | solution.py:17
  199.6 10.6 %collective-permute-start.20 = (f32[32,5,2,128]{3,0,2,1:T(8,128)S(1)}, f32[32,5,2,128]{3,0,2,1:T(8,128)S(1)}, u32[]{:S(2)}, u32[]{:S(2)}) collective-permute-start(f32[32,5,2,128]{3,0,2,1:T(8,128)S(1)} %get-tuple-element.295), channel_id=1, source_target_pairs={{8,0},{16,8},{24,16},{32,24},{40,32},{48,40},{56,48},{64,56},{72,6... | collective-permute-start | bytes 491528 | tf_op jit(solution)/shard_map/ppermute | solution.py:18
  200.9 11.1 %collective-permute-start.21 = (f32[32,5,2,128]{3,0,2,1:T(8,128)S(1)}, f32[32,5,2,128]{3,0,2,1:T(8,128)S(1)}, u32[]{:S(2)}, u32[]{:S(2)}) collective-permute-start(f32[32,5,2,128]{3,0,2,1:T(8,128)S(1)} %get-tuple-element.294), channel_id=1, source_target_pairs={{0,8},{8,16},{16,24},{24,32},{32,40},{40,48},{48,56},{56,64},{64,7... | collective-permute-start | bytes 491528 | tf_op jit(solution)/shard_map/ppermute | solution.py:17
  217.0 8.8 %collective-permute-start.22 = (f32[32,5,20,2]{0,2,3,1:T(8,128)S(1)}, f32[32,5,20,2]{0,2,3,1:T(8,128)}, u32[]{:S(2)}, u32[]{:S(2)}) collective-permute-start(f32[32,5,20,2]{0,2,3,1:T(8,128)S(1)} %copy.285), channel_id=1, source_target_pairs={{1,0},{2,1},{3,2},{4,3},{5,4},{6,5},{7,6},{9,8},{10,9},{11,10},{12... | collective-permute-start | bytes 76808 | tf_op jit(solution)/shard_map/ppermute | solution.py:18
  221.2 7.4 %collective-permute-start.23 = (f32[32,5,20,2]{0,2,3,1:T(8,128)}, f32[32,5,20,2]{0,2,3,1:T(8,128)}, u32[]{:S(2)}, u32[]{:S(2)}) collective-permute-start(f32[32,5,20,2]{0,2,3,1:T(8,128)} %copy.286), channel_id=1, source_target_pairs={{0,1},{1,2},{2,3},{3,4},{4,5},{5,6},{6,7},{8,9},{9,10},{10,11},{11... | collective-permute-start | bytes 76808 | tf_op jit(solution)/shard_map/ppermute | solution.py:17
  (28 other events, 132.4 us)
